TPU v7x, 32 devices: a whole 2x2x4 slice. The times are simulated.
32 devices in a mesh: depth: 2 (over core), tile: 16 (over z, y, x).
Axes of the slice: x: 2, y: 2, z: 4, core: 2. Of those that a mesh axis runs over, the one named last changes fastest.
Arguments:
- object_layer_slices: float32 [2, 2048, 2, 2048], P('depth', 'tile'), may hold values from 0.2 to 1
- probe_wave: bfloat16 [256, 2, 256], replicated, may hold values from -5 to 5
- propagator: bfloat16 [256, 2, 256], replicated, may hold values from -0.25 to 0.25
- positions: int32 [16, 2, 5, 2], P('tile'), may hold values from 0 to 1792, as said below
- counts: int32 [16, 2], P('tile'), may hold values from 2 to 5
- measured: float32 [16, 2, 5, 256, 256], P('tile'), may hold values from 0 to 2
Outputs:
- object_gradient: float32 [2, 2048, 2, 2048], P('depth', 'tile')
Inputs may be any that keep to these rules, and one draw needn't show every extreme that they name: Every window lies inside the object: on tile 0 the first component is 128 or more, on the last tile it is 0 or less; elsewhere it is at most 128, and the second component at most 1792. Slots at or beyond counts[t, b] also hold valid positions. Slots j < counts[t, b] of tile t and micro-batch b are live.
All inputs are finite; a program needn't handle non-finite values.
Results may differ from a plain program's by a relative error of at most 0.013.
Values may be sent and summed in bfloat16 or wider, within the bound.
A program may use at most 192 MiB of HBM per device.

v0:
```python
import math

import jax
import jax.numpy as jnp
import numpy as np
from jax import lax
from jax.experimental import pallas as pl
from jax.experimental.pallas import tpu as pltpu
from jax.sharding import PartitionSpec as P

LANES = 128
CHUNKS = 8
MESH = pl.DeviceIdType.MESH
VMEM = pl.BlockSpec(memory_space=pltpu.VMEM)
SMEM = pl.BlockSpec(memory_space=pltpu.SMEM)
ANY = pl.BlockSpec(memory_space=pl.ANY)
f32, bf16 = jnp.float32, jnp.bfloat16


def dft_block(side):
    index = np.arange(side)
    angles = (index[:, None] * index[None, :] % side) * (2.0 * math.pi / side)
    factor = 1.0 / math.sqrt(side)
    real, imag = np.cos(angles) * factor, -np.sin(angles) * factor
    return np.block([[real, -imag], [imag, real]]).astype(np.float32).astype(bf16)


def route():
    tile, tiles = lax.axis_index("tile"), lax.axis_size("tile")
    odd = lax.rem(tile, 2)
    outward = tile + 2 - 4 * odd
    inward = tile - 2 + 4 * odd
    sends = (outward >= 0) & (outward < tiles)
    takes = (inward >= 0) & (inward < tiles)
    return odd, tile + 1 - 2 * odd, outward, inward, sends, takes


def greet(cores):
    odd, partner, outward, inward, sends, takes = route()
    barrier = pltpu.get_barrier_semaphore()
    pl.semaphore_signal(barrier, inc=1, device_id={"tile": partner}, device_id_type=MESH)
    expected = 1 + sends.astype(jnp.int32) + takes.astype(jnp.int32)
    if cores:
        other = 1 - lax.axis_index("depth")
        pl.semaphore_signal(barrier, inc=1, device_id={"depth": other}, device_id_type=MESH)
        expected = expected + 1

    @pl.when(sends)
    def _():
        pl.semaphore_signal(barrier, inc=1, device_id={"tile": outward}, device_id_type=MESH)

    @pl.when(takes)
    def _():
        pl.semaphore_signal(barrier, inc=1, device_id={"tile": inward}, device_id_type=MESH)

    pl.semaphore_wait(barrier, expected)


def remote(src, dst, sems, slot, target):
    return pltpu.make_async_remote_copy(
        src_ref=src, dst_ref=dst, send_sem=sems.at[0, slot], recv_sem=sems.at[1, slot],
        device_id=target, device_id_type=MESH,
    )


def spot(pos_ref, batch, slot, blocks, wide):
    row, column = pos_ref[0, batch, slot, 0], pos_ref[0, batch, slot, 1]
    block = jnp.minimum(lax.shift_right_logical(column, 7), blocks - wide - 1)
    return row, block, column - block * LANES


def main_kernel(
    pos_ref, count_ref, mine_ref, meas_ref, probe_ref, prop_ref, dft_ref, dft_t_ref,
    own_ref, recv_ref,
    near, far, ext, send_win, keep_win, recv_win, other, meas, prop, prop_t,
    near_sem, far_sem, win_sem, patch_sem, meas_sem,
):
    odd, partner, outward, inward, sends, takes = route()
    section = lax.axis_index("depth")
    core = {"depth": 1 - section}
    blocks, _, rows, _ = mine_ref.shape
    margin = near.shape[2]
    per = blocks // CHUNKS
    slots, side = own_ref.shape[0], own_ref.shape[2]
    wide = side // LANES
    greet(True)

    def near_copy(q):
        span = pl.ds(q * per, per)
        return remote(mine_ref.at[span], near.at[span], near_sem, q, {"tile": partner})

    def far_copy(q):
        span = pl.ds(q * per, per)
        return remote(near.at[span], far.at[span], far_sem, q, {"tile": outward})

    def loop(count, body):
        def step(i, carry):
            body(i)
            return carry

        lax.fori_loop(0, count, step, 0)

    loop(CHUNKS, lambda q: near_copy(q).start())
    meas_copy = pltpu.make_async_copy(meas_ref.at[0, section], meas, meas_sem)
    meas_copy.start()

    real, imag = prop_ref[0].astype(f32), prop_ref[1].astype(f32)
    real_t, imag_t = real.T, imag.T
    for ref, re, up, down in ((prop, real, -imag, imag), (prop_t, real_t, imag_t, -imag_t)):
        ref[:side, :side] = re.astype(bf16)
        ref[:side, side:] = up.astype(bf16)
        ref[side:, :side] = down.astype(bf16)
        ref[side:, side:] = re.astype(bf16)

    near_row = pl.multiple_of((1 - odd) * (margin + rows), 8)
    far_row = pl.multiple_of(odd * (margin + rows), 8)

    def fill(q, source, row):
        span = pl.ds(q * per, per)
        ext[span, :, pl.ds(row, source.shape[2]), :] = source[span].astype(f32)

    loop(CHUNKS, lambda q: fill(q, mine_ref, margin))

    def pass_on(q):
        near_copy(q).wait_recv()

        @pl.when(sends)
        def _():
            far_copy(q).start()

        fill(q, near, near_row)

    loop(CHUNKS, pass_on)

    def take(q):
        @pl.when(takes)
        def _():
            far_copy(q).wait_recv()
            fill(q, far, far_row)

        @pl.when(jnp.logical_not(takes))
        def _():
            span = pl.ds(q * per, per)
            ext[span, :, pl.ds(far_row, margin), :] = jnp.zeros((per, 2, margin, LANES), f32)

    loop(CHUNKS, take)

    lane = lax.broadcasted_iota(jnp.int32, (side, LANES), 1)

    def cut(out_ref, batch, slot):
        row, block, shift = spot(pos_ref, batch, slot, blocks, wide)
        turn = lax.rem(LANES - shift, LANES)
        inside = lane < LANES - shift
        for part in range(2):
            pieces = [
                pltpu.roll(ext[block + k, part, pl.ds(row, side), :], turn, axis=1)
                for k in range(wide + 1)
            ]
            for k in range(wide):
                out_ref[slot, part, :, k * LANES : (k + 1) * LANES] = jnp.where(
                    inside, pieces[k], pieces[k + 1]
                ).astype(bf16)

    def window_copy(slot):
        return remote(send_win.at[slot], recv_win.at[slot], win_sem, slot, core)

    def patch_copy(slot):
        return remote(other.at[slot], recv_ref.at[slot], patch_sem, slot, core)

    def cut_send(slot):
        cut(send_win, 1 - section, slot)

        @pl.when(slot > 0)
        def _():
            window_copy(slot - 1).start()

    loop(slots, cut_send)

    def cut_keep(slot):
        cut(keep_win, section, slot)

        @pl.when(slot == 0)
        def _():
            window_copy(slots - 1).start()

    loop(slots, cut_keep)
    meas_copy.wait()

    def transform(left, right, real, imag):
        stacked = jnp.concatenate([real.astype(bf16), imag.astype(bf16)], axis=0)
        half = jnp.dot(left[...], stacked, preferred_element_type=f32).astype(bf16)
        across = jnp.concatenate([half[:side], half[side:]], axis=1)
        whole = jnp.dot(across, right[...], preferred_element_type=f32)
        return whole[:, :side], whole[:, side:]

    def rounded(pair):
        return tuple(value.astype(bf16).astype(f32) for value in pair)

    def times(a, b):
        return a[0] * b[0] - a[1] * b[1], a[0] * b[1] + a[1] * b[0]

    def conj_times(a, b):
        return a[0] * b[0] + a[1] * b[1], a[0] * b[1] - a[1] * b[0]

    def wave(slot):
        window_copy(slot).wait_recv()
        first = section == 0
        live = (slot < count_ref[0, section]).astype(f32)

        def field(part):
            a, b = keep_win[slot, part], recv_win[slot, part]
            return jnp.where(first, a, b).astype(f32), jnp.where(first, b, a).astype(f32)

        (x0r, x1r), (x0i, x1i) = field(0), field(1)
        x0, x1 = (x0r, x0i), (x1r, x1i)
        psi0 = (probe_ref[0].astype(f32), probe_ref[1].astype(f32))
        psi1 = rounded(transform(prop, prop_t, *times(psi0, x0)))
        wave_far = transform(dft_ref, dft_t_ref, *times(psi1, x1))
        misfit = live * (wave_far[0] * wave_far[0] + wave_far[1] * wave_far[1] - meas[slot])
        g1 = rounded(transform(dft_t_ref, dft_ref, misfit * wave_far[0], misfit * wave_far[1]))
        patch1 = conj_times(psi1, g1)
        g0 = rounded(transform(prop_t, prop, *conj_times(x1, g1)))
        patch0 = conj_times(psi0, g0)
        for part in range(2):
            a, b = patch0[part].astype(bf16), patch1[part].astype(bf16)
            own_ref[slot, part] = jnp.where(first, a, b)
            other[slot, part] = jnp.where(first, b, a)

        @pl.when(slot > 0)
        def _():
            patch_copy(slot - 1).start()

    loop(slots, wave)

    def settle(q):
        near_copy(q).wait_send()

        @pl.when(sends)
        def _():
            far_copy(q).wait_send()

    loop(CHUNKS, settle)
    loop(slots, lambda slot: window_copy(slot).wait_send())
    patch_copy(slots - 1).start()
    loop(slots, lambda slot: patch_copy(slot).wait())


def add_kernel(pos_ref, own_ref, recv_ref, inner_ref, near_ref, far_ref, total):
    odd = route()[0]
    section = lax.axis_index("depth")
    total[...] = jnp.zeros_like(total)
    slots, side = own_ref.shape[0], own_ref.shape[2]
    wide = side // LANES
    lane = lax.broadcasted_iota(jnp.int32, (side, LANES), 1)

    def add(patch_ref, batch):
        def body(slot, carry):
            row, block, shift = spot(pos_ref, batch, slot, total.shape[0], wide)
            turn = lax.rem(shift, LANES)
            inside = lane >= shift
            for part in range(2):
                pieces = [
                    pltpu.roll(
                        patch_ref[slot, part, :, k * LANES : (k + 1) * LANES].astype(f32),
                        turn,
                        axis=1,
                    )
                    for k in range(wide)
                ]
                pieces = [jnp.zeros_like(pieces[0])] + pieces + [jnp.zeros_like(pieces[0])]
                for k in range(wide + 1):
                    total[block + k, part, pl.ds(row, side), :] += jnp.where(
                        inside, pieces[k + 1], pieces[k]
                    )
            return carry

        lax.fori_loop(0, slots, body, 0)

    add(own_ref, section)
    add(recv_ref, 1 - section)
    margin, rows = near_ref.shape[2], inner_ref.shape[2]
    near_row = pl.multiple_of((1 - odd) * (margin + rows), 8)
    far_row = pl.multiple_of(odd * (margin + rows), 8)
    inner_ref[...] = total[:, :, pl.ds(margin, rows), :]
    near_ref[...] = total[:, :, pl.ds(near_row, margin), :].astype(bf16)
    far_ref[...] = total[:, :, pl.ds(far_row, margin), :].astype(bf16)


def home_kernel(inner_ref, near_ref, far_ref, out_ref, passed, joined, arrived, far_sem, near_sem):
    odd, partner, outward, inward, sends, takes = route()
    blocks = inner_ref.shape[0]
    per = blocks // CHUNKS
    greet(False)

    def loop(body):
        def step(i, carry):
            body(i)
            return carry

        lax.fori_loop(0, CHUNKS, step, 0)

    def far_copy(q):
        span = pl.ds(q * per, per)
        return remote(far_ref.at[span], passed.at[span], far_sem, q, {"tile": inward})

    def near_copy(q):
        span = pl.ds(q * per, per)
        return remote(joined.at[span], arrived.at[span], near_sem, q, {"tile": partner})

    @pl.when(takes)
    def _():
        loop(lambda q: far_copy(q).start())

    def join(q):
        span = pl.ds(q * per, per)

        @pl.when(sends)
        def _():
            far_copy(q).wait_recv()
            joined[span] = (near_ref[span].astype(f32) + passed[span].astype(f32)).astype(bf16)

        @pl.when(jnp.logical_not(sends))
        def _():
            joined[span] = near_ref[span]

        near_copy(q).start()

    loop(join)

    def finish(q):
        span = pl.ds(q * per, per)
        near_copy(q).wait_recv()
        out_ref[span] = inner_ref[span] + arrived[span].astype(f32)

    loop(finish)

    def settle(q):
        near_copy(q).wait_send()

        @pl.when(takes)
        def _():
            far_copy(q).wait_send()

    loop(settle)


def local(object_layer_slices, probe_wave, propagator, positions, counts, measured):
    side = probe_wave.shape[0]
    _, rows, _, columns = object_layer_slices.shape
    slots = positions.shape[2]
    margin = side // 2
    sections, tiles = lax.axis_size("depth"), lax.axis_size("tile")
    assert sections == 2 and positions.shape[1] == sections and object_layer_slices.shape[0] == 1
    assert tiles % 2 == 0 and rows == margin
    blocks = columns // LANES
    extent = (blocks, 2, rows + 2 * margin, LANES)
    tile_shape, window_shape = (blocks, 2, margin, LANES), (slots, 2, side, side)
    tile_bf16 = jax.ShapeDtypeStruct(tile_shape, bf16)
    tile_f32 = jax.ShapeDtypeStruct(tile_shape, f32)
    window = jax.ShapeDtypeStruct(window_shape, bf16)

    mine = (
        object_layer_slices[0].astype(bf16).reshape(rows, 2, blocks, LANES).transpose(2, 1, 0, 3)
    )
    dft = dft_block(side)
    own, recv = pl.pallas_call(
        main_kernel,
        out_shape=(window, window),
        in_specs=[SMEM, SMEM, VMEM, ANY, VMEM, VMEM, VMEM, VMEM],
        out_specs=(VMEM, VMEM),
        scratch_shapes=[pltpu.VMEM(tile_shape, bf16)] * 2
        + [pltpu.VMEM(extent, f32)]
        + [pltpu.VMEM(window_shape, bf16)] * 4
        + [pltpu.VMEM((slots, side, side), f32)]
        + [pltpu.VMEM((2 * side, 2 * side), bf16)] * 2
        + [pltpu.SemaphoreType.DMA((2, CHUNKS))] * 2
        + [pltpu.SemaphoreType.DMA((2, slots))] * 2
        + [pltpu.SemaphoreType.DMA],
        compiler_params=pltpu.CompilerParams(collective_id=0, has_side_effects=True),
        name="waves",
    )(
        positions, counts, mine, measured, probe_wave.transpose(1, 0, 2),
        propagator.transpose(1, 0, 2), jnp.asarray(dft), jnp.asarray(np.ascontiguousarray(dft.T)),
    )
    inner, near, far = pl.pallas_call(
        add_kernel,
        out_shape=(tile_f32, tile_bf16, tile_bf16),
        in_specs=[SMEM, VMEM, VMEM],
        out_specs=(VMEM, VMEM, VMEM),
        scratch_shapes=[pltpu.VMEM(extent, f32)],
        name="add",
    )(positions, own, recv)
    total = pl.pallas_call(
        home_kernel,
        out_shape=tile_f32,
        in_specs=[VMEM] * 3,
        out_specs=VMEM,
        scratch_shapes=[pltpu.VMEM(tile_shape, bf16)] * 3
        + [pltpu.SemaphoreType.DMA((2, CHUNKS))] * 2,
        compiler_params=pltpu.CompilerParams(collective_id=1, has_side_effects=True),
        name="home",
    )(inner, near, far)
    return total.transpose(2, 1, 0, 3).reshape(1, rows, 2, columns)


def solution(mesh):
    placed = (
        P("depth", "tile", None, None),
        P(),
        P(),
        P("tile", None, None, None),
        P("tile", None),
        P("tile", None, None, None, None),
    )
    return jax.shard_map(
        local, mesh=mesh, in_specs=placed, out_specs=P("depth", "tile", None, None), check_vma=False
    )
```

profile of v0, /device:TPU:0, one launch (start us, length us, event | category | flops | bytes accessed | tf_op | source)
XLA Modules:
  0.0 104.3 jit_solution(11350450372470794154)
XLA Ops:
  0.0 1.4 %copy.18.pos_ref = s32[1,2,5,2]{3,2,1,0:T(8,128)} copy(s32[1,2,5,2]{2,3,1,0:T(2,128)} %param.11) | data formatting | bytes 160 | tf_op args[3]
  1.4 1.9 %copy_bitcast_fusion = (bf16[2,256,256]{2,1,0:T(8,128)(2,1)}, bf16[2,256,256]{2,1,0:T(8,128)(2,1)}) fusion(bf16[256,2,256]{2,1,0:T(2,128)(2,1)} %param.10, bf16[256,2,256]{2,1,0:T(2,128)(2,1)} %param.9), kind=kLoop, calls=%fused_computation | loop fusion | bytes 1048576 | tf_op jit(solution)/shard_map/transpose | solution.py:383
  3.3 2.7 %copy.13 = bf16[1,128,2,2048]{1,3,2,0:T(8,128)(2,1)S(1)} copy(f32[1,128,2,2048]{3,2,1,0:T(2,128)} %param.8) | data formatting | bytes 3145728 | tf_op args[0]
  5.9 1.3 %copy.14 = bf16[128,2,16,128]{3,0,1,2:T(8,128)(2,1)} copy(bf16[128,2,16,128]{0,3,2,1:T(8,128)(2,1)S(1)} %bitcast.10) | data formatting | bytes 2097152 | tf_op jit(solution)/shard_map/convert_element_type | solution.py:363
  7.2 48.4 %waves.1 = (bf16[5,2,256,256]{3,2,1,0:T(8,128)(2,1)}, bf16[5,2,256,256]{3,2,1,0:T(8,128)(2,1)}) custom-call(s32[1,2,5,2]{3,2,1,0:T(8,128)} %copy.18.pos_ref, s32[1,2]{1,0:T(1,128)} %count_ref.1, bf16[16,2,128,128]{3,2,1,0:T(8,128)(2,1)} %bitcast.11, f32[1,2,5,256,256]{4,3,2,1,0:T(8,128)} %meas_ref.1, bf16[2,256,256]{2,1,0:T(8,128)(2,1)} %get-tuple-element.16.probe_ref, ...), custom_call_target="tpu_custom_call" | custom-call | tf_op jit(solution)/shard_map/waves/pallas_call | solution.py:366
  55.6 5.8 %add.1 = (f32[16,2,128,128]{3,2,1,0:T(8,128)}, bf16[16,2,128,128]{3,2,1,0:T(8,128)(2,1)}, bf16[16,2,128,128]{3,2,1,0:T(8,128)(2,1)}) custom-call(s32[1,2,5,2]{3,2,1,0:T(8,128)} %copy.18.pos_ref, bf16[5,2,256,256]{3,2,1,0:T(8,128)(2,1)} %get-tuple-element.10.own_ref, bf16[5,2,256,256]{3,2,1,0:T(8,128)(2,1)} %get-tuple-element.11.recv_ref), custom_call_target="tpu_custom_call" | custom-call | tf_op jit(solution)/shard_map/add/pallas_call | solution.py:385
  61.4 38.6 %home.1 = f32[16,2,128,128]{3,2,1,0:T(8,128)} custom-call(f32[16,2,128,128]{3,2,1,0:T(8,128)} %get-tuple-element.12.inner_ref, bf16[16,2,128,128]{3,2,1,0:T(8,128)(2,1)} %get-tuple-element.13.near_ref, bf16[16,2,128,128]{3,2,1,0:T(8,128)(2,1)} %get-tuple-element.14.far_ref), custom_call_target="tpu_custom_call" | custom-call | tf_op jit(solution)/shard_map/home/pallas_call | solution.py:393
  100.0 1.9 %copy.19 = f32[128,2,16,128]{0,3,2,1:T(8,128)S(1)} copy(f32[128,2,16,128]{3,0,1,2:T(8,128)} %bitcast.8) | data formatting | bytes 4194304 | tf_op jit(solution)/shard_map/transpose | solution.py:403
  102.0 2.3 %copy.20 = f32[1,128,2,2048]{3,2,1,0:T(2,128)} copy(f32[1,128,2,2048]{1,3,2,0:T(8,128)S(1)} %bitcast.9) | data formatting | bytes 4194304 | tf_op jit(solution)/shard_map/reshape | solution.py:403
where the time goes:
time: 105 us; the launch traced here: 104 us
  Pallas kernels  92.8 us (88%)
  local copies, waits for them, and re-layouts  11.5 us (11%)
    pallas_call x1, Pallas kernels, local(): pl.pallas_call(main_kernel, out_shape=(window, window), in_specs=[SMEM, S...  48.4 us
    pallas_call x1, Pallas kernels, local(): pl.pallas_call(home_kernel, out_shape=tile_f32, in_specs=[VMEM] * 3, out_...  38.6 us
    pallas_call x1, Pallas kernels, local(): pl.pallas_call(add_kernel, out_shape=(tile_f32, tile_bf16, tile_bf16), in...  5.79 us
    unnamed x2, local copies, waits for them, and re-layouts  4.03 us
    reshape x1, local copies, waits for them, and re-layouts, local(): return total.transpose(2, 1, 0, 3).reshape(1, rows, 2, columns)  2.33 us

commit v1 on v0

--- a/solution.py
+++ b/solution.py
@@ -9,11 +9,11 @@
 from jax.sharding import PartitionSpec as P
 
 LANES = 128
-CHUNKS = 8
+CHUNKS = 16
 MESH = pl.DeviceIdType.MESH
 VMEM = pl.BlockSpec(memory_space=pltpu.VMEM)
 SMEM = pl.BlockSpec(memory_space=pltpu.SMEM)
-ANY = pl.BlockSpec(memory_space=pl.ANY)
+HBM = pl.BlockSpec(memory_space=pltpu.HBM)
 f32, bf16 = jnp.float32, jnp.bfloat16
 
 
@@ -70,24 +70,29 @@
 
 
 def main_kernel(
-    pos_ref, count_ref, mine_ref, meas_ref, probe_ref, prop_ref, dft_ref, dft_t_ref,
+    pos_ref, count_ref, object_ref, meas_ref, probe_ref, prop_ref, dft_ref, dft_t_ref,
     own_ref, recv_ref,
-    near, far, ext, send_win, keep_win, recv_win, other, meas, prop, prop_t,
+    mine, near, far, ext, send_win, keep_win, recv_win, other, meas, prop, prop_t,
     near_sem, far_sem, win_sem, patch_sem, meas_sem,
 ):
     odd, partner, outward, inward, sends, takes = route()
     section = lax.axis_index("depth")
     core = {"depth": 1 - section}
-    blocks, _, rows, _ = mine_ref.shape
+    blocks, _, rows, _ = mine.shape
     margin = near.shape[2]
     per = blocks // CHUNKS
     slots, side = own_ref.shape[0], own_ref.shape[2]
     wide = side // LANES
+    for block in range(blocks):
+        for part in range(2):
+            values = object_ref[pl.ds(2 * block + part, rows, stride=2 * blocks), :]
+            mine[block, part] = values.astype(bf16)
+            ext[block, part, pl.ds(margin, rows), :] = values.astype(bf16).astype(f32)
     greet(True)
 
     def near_copy(q):
         span = pl.ds(q * per, per)
-        return remote(mine_ref.at[span], near.at[span], near_sem, q, {"tile": partner})
+        return remote(mine.at[span], near.at[span], near_sem, q, {"tile": partner})
 
     def far_copy(q):
         span = pl.ds(q * per, per)
@@ -118,8 +123,6 @@
     def fill(q, source, row):
         span = pl.ds(q * per, per)
         ext[span, :, pl.ds(row, source.shape[2]), :] = source[span].astype(f32)
-
-    loop(CHUNKS, lambda q: fill(q, mine_ref, margin))
 
     def pass_on(q):
         near_copy(q).wait_recv()
@@ -186,51 +189,68 @@
     loop(slots, cut_keep)
     meas_copy.wait()
 
-    def transform(left, right, real, imag):
-        stacked = jnp.concatenate([real.astype(bf16), imag.astype(bf16)], axis=0)
+    def rounded(whole):
+        return whole[:, :side].astype(bf16), whole[:, side:].astype(bf16)
+
+    def times(a, b):
+        a, b = [x.astype(f32) for x in a], [x.astype(f32) for x in b]
+        return a[0] * b[0] - a[1] * b[1], a[0] * b[1] + a[1] * b[0]
+
+    def conj_times(a, b):
+        a, b = [x.astype(f32) for x in a], [x.astype(f32) for x in b]
+        return a[0] * b[0] + a[1] * b[1], a[0] * b[1] - a[1] * b[0]
+
+    first = section == 0
+
+    def left_half(left, pair):
+        stacked = jnp.concatenate([pair[0].astype(bf16), pair[1].astype(bf16)], axis=0)
         half = jnp.dot(left[...], stacked, preferred_element_type=f32).astype(bf16)
-        across = jnp.concatenate([half[:side], half[side:]], axis=1)
-        whole = jnp.dot(across, right[...], preferred_element_type=f32)
-        return whole[:, :side], whole[:, side:]
-
-    def rounded(pair):
-        return tuple(value.astype(bf16).astype(f32) for value in pair)
-
-    def times(a, b):
-        return a[0] * b[0] - a[1] * b[1], a[0] * b[1] + a[1] * b[0]
-
-    def conj_times(a, b):
-        return a[0] * b[0] + a[1] * b[1], a[0] * b[1] - a[1] * b[0]
+        return jnp.concatenate([half[:side], half[side:]], axis=1)
+
+    def right_half(right, across):
+        return jnp.dot(across, right[...], preferred_element_type=f32)
+
+    def slice_window(slot, number):
+        return [
+            jnp.where(first, keep_win[slot, part], recv_win[slot, part])
+            if number == 0
+            else jnp.where(first, recv_win[slot, part], keep_win[slot, part])
+            for part in range(2)
+        ]
 
     def wave(slot):
         window_copy(slot).wait_recv()
-        first = section == 0
         live = (slot < count_ref[0, section]).astype(f32)
-
-        def field(part):
-            a, b = keep_win[slot, part], recv_win[slot, part]
-            return jnp.where(first, a, b).astype(f32), jnp.where(first, b, a).astype(f32)
-
-        (x0r, x1r), (x0i, x1i) = field(0), field(1)
-        x0, x1 = (x0r, x0i), (x1r, x1i)
-        psi0 = (probe_ref[0].astype(f32), probe_ref[1].astype(f32))
-        psi1 = rounded(transform(prop, prop_t, *times(psi0, x0)))
-        wave_far = transform(dft_ref, dft_t_ref, *times(psi1, x1))
-        misfit = live * (wave_far[0] * wave_far[0] + wave_far[1] * wave_far[1] - meas[slot])
-        g1 = rounded(transform(dft_t_ref, dft_ref, misfit * wave_far[0], misfit * wave_far[1]))
+        psi0 = (probe_ref[0], probe_ref[1])
+        across = left_half(prop, times(psi0, slice_window(slot, 0)))
+        yield
+        psi1 = rounded(right_half(prop_t, across))
+        yield
+        across = left_half(dft_ref, times(psi1, slice_window(slot, 1)))
+        yield
+        whole = right_half(dft_t_ref, across)
+        re, im = whole[:, :side], whole[:, side:]
+        misfit = live * (re * re + im * im - meas[slot])
+        yield
+        across = left_half(dft_t_ref, (misfit * re, misfit * im))
+        yield
+        g1 = rounded(right_half(dft_ref, across))
+        yield
+        across = left_half(prop_t, conj_times(slice_window(slot, 1), g1))
         patch1 = conj_times(psi1, g1)
-        g0 = rounded(transform(prop_t, prop, *conj_times(x1, g1)))
+        yield
+        g0 = rounded(right_half(prop, across))
         patch0 = conj_times(psi0, g0)
         for part in range(2):
             a, b = patch0[part].astype(bf16), patch1[part].astype(bf16)
             own_ref[slot, part] = jnp.where(first, a, b)
             other[slot, part] = jnp.where(first, b, a)
-
-        @pl.when(slot > 0)
-        def _():
+        if slot > 0:
             patch_copy(slot - 1).start()
 
-    loop(slots, wave)
+    running = [wave(slot) for slot in range(slots)]
+    while running:
+        running = [chain for chain in running if next(chain, True) is None]
 
     def settle(q):
         near_copy(q).wait_send()
@@ -327,12 +347,14 @@
 
     loop(join)
 
-    def finish(q):
-        span = pl.ds(q * per, per)
+    rows = inner_ref.shape[2]
+    for q in range(CHUNKS):
         near_copy(q).wait_recv()
-        out_ref[span] = inner_ref[span] + arrived[span].astype(f32)
-
-    loop(finish)
+        for block in range(q * per, (q + 1) * per):
+            for part in range(2):
+                out_ref[pl.ds(2 * block + part, rows, stride=2 * blocks), :] = inner_ref[
+                    block, part
+                ] + arrived[block, part].astype(f32)
 
     def settle(q):
         near_copy(q).wait_send()
@@ -359,16 +381,16 @@
     tile_f32 = jax.ShapeDtypeStruct(tile_shape, f32)
     window = jax.ShapeDtypeStruct(window_shape, bf16)
 
-    mine = (
-        object_layer_slices[0].astype(bf16).reshape(rows, 2, blocks, LANES).transpose(2, 1, 0, 3)
-    )
+    lines = jax.ShapeDtypeStruct((rows * blocks * 2, LANES), f32)
+    view = object_layer_slices.reshape(rows, 2, blocks, LANES).transpose(0, 2, 1, 3)
+    view = view.reshape(lines.shape)
     dft = dft_block(side)
     own, recv = pl.pallas_call(
         main_kernel,
         out_shape=(window, window),
-        in_specs=[SMEM, SMEM, VMEM, ANY, VMEM, VMEM, VMEM, VMEM],
+        in_specs=[SMEM, SMEM, VMEM, HBM, VMEM, VMEM, VMEM, VMEM],
         out_specs=(VMEM, VMEM),
-        scratch_shapes=[pltpu.VMEM(tile_shape, bf16)] * 2
+        scratch_shapes=[pltpu.VMEM(tile_shape, bf16)] * 3
         + [pltpu.VMEM(extent, f32)]
         + [pltpu.VMEM(window_shape, bf16)] * 4
         + [pltpu.VMEM((slots, side, side), f32)]
@@ -376,10 +398,12 @@
         + [pltpu.SemaphoreType.DMA((2, CHUNKS))] * 2
         + [pltpu.SemaphoreType.DMA((2, slots))] * 2
         + [pltpu.SemaphoreType.DMA],
-        compiler_params=pltpu.CompilerParams(collective_id=0, has_side_effects=True),
+        compiler_params=pltpu.CompilerParams(
+            collective_id=0, has_side_effects=True, vmem_limit_bytes=44 << 20
+        ),
         name="waves",
     )(
-        positions, counts, mine, measured, probe_wave.transpose(1, 0, 2),
+        positions, counts, view, measured, probe_wave.transpose(1, 0, 2),
         propagator.transpose(1, 0, 2), jnp.asarray(dft), jnp.asarray(np.ascontiguousarray(dft.T)),
     )
     inner, near, far = pl.pallas_call(
@@ -388,19 +412,23 @@
         in_specs=[SMEM, VMEM, VMEM],
         out_specs=(VMEM, VMEM, VMEM),
         scratch_shapes=[pltpu.VMEM(extent, f32)],
+        compiler_params=pltpu.CompilerParams(vmem_limit_bytes=24 << 20),
         name="add",
     )(positions, own, recv)
     total = pl.pallas_call(
         home_kernel,
-        out_shape=tile_f32,
+        out_shape=lines,
         in_specs=[VMEM] * 3,
         out_specs=VMEM,
         scratch_shapes=[pltpu.VMEM(tile_shape, bf16)] * 3
         + [pltpu.SemaphoreType.DMA((2, CHUNKS))] * 2,
-        compiler_params=pltpu.CompilerParams(collective_id=1, has_side_effects=True),
+        compiler_params=pltpu.CompilerParams(
+            collective_id=1, has_side_effects=True, vmem_limit_bytes=20 << 20
+        ),
         name="home",
     )(inner, near, far)
-    return total.transpose(2, 1, 0, 3).reshape(1, rows, 2, columns)
+    total = total.reshape(rows, blocks, 2, LANES).transpose(0, 2, 1, 3)
+    return total.reshape(1, rows, 2, columns)
 
 
 def solution(mesh):

time: 105 us -> 88.6 us (0.84)
  Pallas kernels: 92.8 us -> 79 us
  local copies, waits for them, and re-layouts: 11.5 us -> 9.26 us
    pallas_call x1, Pallas kernels: 48.4 us -> 42.8 us  [local(): pl.pallas_call(main_kernel, out_shape=(window, window), in_specs=[SMEM, S...]
    pallas_call x1, Pallas kernels: 38.6 us -> 33.2 us  [local(): pl.pallas_call(home_kernel, out_shape=lines, in_specs=[VMEM] * 3, out_spe...]
    unnamed x2 -> x12, local copies, waits for them, and re-layouts: 4.03 us -> 8.16 us
    pallas_call x1, Pallas kernels: 5.79 us -> 2.95 us  [local(): pl.pallas_call(add_kernel, out_shape=(tile_f32, tile_bf16, tile_bf16), in...]
    reshape x1 -> x0, local copies, waits for them, and re-layouts: 2.33 us -> none  [local(): return total.transpose(2, 1, 0, 3).reshape(1, rows, 2, columns)]
    transpose x1 -> x0, local copies, waits for them, and re-layouts: 1.94 us -> none  [local(): return total.transpose(2, 1, 0, 3).reshape(1, rows, 2, columns)]
    convert_element_type x1 -> x0, local copies, waits for them, and re-layouts: 1.31 us -> none  [local(): object_layer_slices[0].astype(bf16).reshape(rows, 2, blocks, LANES)]
where the time goes in v1:
time: 88.6 us; the launch traced here: 88.3 us
  Pallas kernels  79 us (89%)
  local copies, waits for them, and re-layouts  9.26 us (10%)
    pallas_call x1, Pallas kernels, local(): pl.pallas_call(main_kernel, out_shape=(window, window), in_specs=[SMEM, S...  42.8 us
    pallas_call x1, Pallas kernels, local(): pl.pallas_call(home_kernel, out_shape=lines, in_specs=[VMEM] * 3, out_spe...  33.2 us
    unnamed x12, local copies, waits for them, and re-layouts  8.16 us
    pallas_call x1, Pallas kernels, local(): pl.pallas_call(add_kernel, out_shape=(tile_f32, tile_bf16, tile_bf16), in...  2.95 us

profile of v1, /device:TPU:0, one launch (start us, length us, event | category | flops | bytes accessed | tf_op | source)
XLA Modules:
  0.0 88.3 jit_solution(4956205142840505360)
XLA Ops:
  0.0 0.8 copy.13.pos_ref
  0.8 1.1 %copy_bitcast_fusion = (bf16[2,256,256]{2,1,0:T(8,128)(2,1)S(1)}, bf16[2,256,256]{2,1,0:T(8,128)(2,1)S(1)}) fusion(bf16[256,2,256]{2,1,0:T(2,128)(2,1)} %param.10, bf16[256,2,256]{2,1,0:T(2,128)(2,1)} %param.9), kind=kLoop, calls=%fused_computation | loop fusion | bytes 1048576 | tf_op jit(solution)/shard_map/transpose | solution.py:407
  1.9 0.0 copy-start
  1.9 1.7 %copy-done = f32[1,2,5,256,256]{4,3,2,1,0:T(8,128)S(1)} copy-done((f32[1,2,5,256,256]{4,3,2,1,0:T(8,128)S(1)}, f32[1,2,5,256,256]{4,3,2,1,0:T(8,128)}, u32[]{:S(2)}) %copy-start) | copy-done | bytes 2621464
  3.6 0.0 copy-start.1
  3.6 1.6 %copy-done.1 = f32[1,128,2,2048]{3,2,1,0:T(2,128)S(1)} copy-done((f32[1,128,2,2048]{3,2,1,0:T(2,128)S(1)}, f32[1,128,2,2048]{3,2,1,0:T(2,128)}, u32[]{:S(2)}) %copy-start.1) | copy-done | bytes 2097176
  5.2 0.0 copy-start.2
  5.2 1.0 %copy-done.2 = bf16[512,512]{1,0:T(8,128)(2,1)S(1)} copy-done((bf16[512,512]{1,0:T(8,128)(2,1)S(1)}, bf16[512,512]{1,0:T(8,128)(2,1)}, u32[]{:S(2)}) %copy-start.2) | copy-done | bytes 524312
  6.3 0.0 copy-start.3
  6.3 1.0 %copy-done.3 = bf16[512,512]{1,0:T(8,128)(2,1)S(1)} copy-done((bf16[512,512]{1,0:T(8,128)(2,1)S(1)}, bf16[512,512]{1,0:T(8,128)(2,1)}, u32[]{:S(2)}) %copy-start.3) | copy-done | bytes 524312
  7.3 0.0 copy-start.4
  7.3 0.7 copy-done.4
  8.0 42.8 %waves.1 = (bf16[5,2,256,256]{3,2,1,0:T(8,128)(2,1)S(1)}, bf16[5,2,256,256]{3,2,1,0:T(8,128)(2,1)S(1)}) custom-call(s32[1,2,5,2]{3,2,1,0:T(8,128)S(1)} %copy.13.pos_ref, s32[1,2]{1,0:T(1,128)S(1)} %copy-done.4, f32[4096,128]{1,0:T(8,128)S(1)} %bitcast.15, f32[1,2,5,256,256]{4,3,2,1,0:T(8,128)S(1)} %copy-done, ...), custom_call_target="tpu_custom_call" | custom-call | tf_op jit(solution)/shard_map/waves/pallas_call | solution.py:388
  50.7 3.0 %add.1 = (f32[16,2,128,128]{3,2,1,0:T(8,128)S(1)}, bf16[16,2,128,128]{3,2,1,0:T(8,128)(2,1)S(1)}, bf16[16,2,128,128]{3,2,1,0:T(8,128)(2,1)S(1)}) custom-call(s32[1,2,5,2]{3,2,1,0:T(8,128)S(1)} %copy.13.pos_ref, bf16[5,2,256,256]{3,2,1,0:T(8,128)(2,1)S(1)} %get-tuple-element.10.own_ref, bf16[5,2,256,256]{3,2,1,0:T(8,128)(2,1)S(1)} %get-tuple-element.11.recv_ref), custom_call_target="tpu_custom_call" | custom-call | tf_op jit(solution)/shard_map/add/pallas_call | solution.py:409
  53.7 33.2 %home.1 = f32[4096,128]{1,0:T(8,128)S(1)} custom-call(f32[16,2,128,128]{3,2,1,0:T(8,128)S(1)} %get-tuple-element.12.inner_ref, bf16[16,2,128,128]{3,2,1,0:T(8,128)(2,1)S(1)} %get-tuple-element.13.near_ref, bf16[16,2,128,128]{3,2,1,0:T(8,128)(2,1)S(1)} %get-tuple-element.14.far_ref), custom_call_target="tpu_custom_call" | custom-call | tf_op jit(solution)/shard_map/home/pallas_call | solution.py:418
  86.9 1.3 %copy.18 = f32[1,128,2,2048]{3,2,1,0:T(2,128)} copy(f32[1,128,2,2048]{3,2,1,0:T(2,128)S(1)} %bitcast.14) | data formatting | bytes 4194304
Async XLA Ops:
  1.9 1.7 %copy-start = (f32[1,2,5,256,256]{4,3,2,1,0:T(8,128)S(1)}, f32[1,2,5,256,256]{4,3,2,1,0:T(8,128)}, u32[]{:S(2)}) copy-start(f32[1,2,5,256,256]{4,3,2,1,0:T(8,128)} %meas_ref.1) | copy-start | bytes 7864324
  3.6 1.6 %copy-start.1 = (f32[1,128,2,2048]{3,2,1,0:T(2,128)S(1)}, f32[1,128,2,2048]{3,2,1,0:T(2,128)}, u32[]{:S(2)}) copy-start(f32[1,128,2,2048]{3,2,1,0:T(2,128)} %param.8) | copy-start | bytes 6291460
  5.2 1.0 %copy-start.2 = (bf16[512,512]{1,0:T(8,128)(2,1)S(1)}, bf16[512,512]{1,0:T(8,128)(2,1)}, u32[]{:S(2)}) copy-start(bf16[512,512]{1,0:T(8,128)(2,1)} %constant.5.clone.dft_t_ref) | copy-start | bytes 1572868
  6.3 1.0 %copy-start.3 = (bf16[512,512]{1,0:T(8,128)(2,1)S(1)}, bf16[512,512]{1,0:T(8,128)(2,1)}, u32[]{:S(2)}) copy-start(bf16[512,512]{1,0:T(8,128)(2,1)} %constant.4.clone.dft_ref) | copy-start | bytes 1572868
  7.3 0.7 copy-start.4

commit v2 on v1

--- a/solution.py
+++ b/solution.py
@@ -17,12 +17,12 @@
 f32, bf16 = jnp.float32, jnp.bfloat16
 
 
-def dft_block(side):
+def dft_planes(side):
     index = np.arange(side)
     angles = (index[:, None] * index[None, :] % side) * (2.0 * math.pi / side)
     factor = 1.0 / math.sqrt(side)
-    real, imag = np.cos(angles) * factor, -np.sin(angles) * factor
-    return np.block([[real, -imag], [imag, real]]).astype(np.float32).astype(bf16)
+    planes = np.stack([np.cos(angles) * factor, -np.sin(angles) * factor])
+    return planes.astype(np.float32).astype(bf16)
 
 
 def route():
@@ -70,10 +70,10 @@
 
 
 def main_kernel(
-    pos_ref, count_ref, object_ref, meas_ref, probe_ref, prop_ref, dft_ref, dft_t_ref,
+    pos_ref, count_ref, object_ref, meas_ref, probe_ref, prop_ref, fourier_ref,
     own_ref, recv_ref,
-    mine, near, far, ext, send_win, keep_win, recv_win, other, meas, prop, prop_t,
-    near_sem, far_sem, win_sem, patch_sem, meas_sem,
+    lines, dft_ref, dft_t_ref, mine, near, far, ext, send_win, keep_win, recv_win, other, meas, prop, prop_t,
+    near_sem, far_sem, win_sem, patch_sem, load_sem,
 ):
     odd, partner, outward, inward, sends, takes = route()
     section = lax.axis_index("depth")
@@ -83,11 +83,9 @@
     per = blocks // CHUNKS
     slots, side = own_ref.shape[0], own_ref.shape[2]
     wide = side // LANES
-    for block in range(blocks):
-        for part in range(2):
-            values = object_ref[pl.ds(2 * block + part, rows, stride=2 * blocks), :]
-            mine[block, part] = values.astype(bf16)
-            ext[block, part, pl.ds(margin, rows), :] = values.astype(bf16).astype(f32)
+    object_copy = pltpu.make_async_copy(object_ref, lines, load_sem.at[0])
+    object_copy.start()
+    meas_copy = pltpu.make_async_copy(meas_ref.at[0, section], meas, load_sem.at[1])
     greet(True)
 
     def near_copy(q):
@@ -105,17 +103,31 @@
 
         lax.fori_loop(0, count, step, 0)
 
-    loop(CHUNKS, lambda q: near_copy(q).start())
-    meas_copy = pltpu.make_async_copy(meas_ref.at[0, section], meas, meas_sem)
+    object_copy.wait()
+    for q in range(CHUNKS):
+        for block in range(q * per, (q + 1) * per):
+            for part in range(2):
+                values = lines[pl.ds(2 * block + part, rows, stride=2 * blocks), :].astype(bf16)
+                mine[block, part] = values
+                ext[block, part, pl.ds(margin, rows), :] = values.astype(f32)
+        if q > 0:
+            near_copy(q - 1).start()
+    near_copy(CHUNKS - 1).start()
     meas_copy.start()
 
-    real, imag = prop_ref[0].astype(f32), prop_ref[1].astype(f32)
-    real_t, imag_t = real.T, imag.T
-    for ref, re, up, down in ((prop, real, -imag, imag), (prop_t, real_t, imag_t, -imag_t)):
-        ref[:side, :side] = re.astype(bf16)
-        ref[:side, side:] = up.astype(bf16)
-        ref[side:, :side] = down.astype(bf16)
-        ref[side:, side:] = re.astype(bf16)
+    def expand(source, block, block_t):
+        real, imag = source[0].astype(f32), source[1].astype(f32)
+        real_t, imag_t = real.T, imag.T
+        for ref, same, up, down in (
+            (block, real, -imag, imag), (block_t, real_t, imag_t, -imag_t)
+        ):
+            ref[:side, :side] = same.astype(bf16)
+            ref[:side, side:] = up.astype(bf16)
+            ref[side:, :side] = down.astype(bf16)
+            ref[side:, side:] = same.astype(bf16)
+
+    expand(prop_ref, prop, prop_t)
+    expand(fourier_ref, dft_ref, dft_t_ref)
 
     near_row = pl.multiple_of((1 - odd) * (margin + rows), 8)
     far_row = pl.multiple_of(odd * (margin + rows), 8)
@@ -384,27 +396,28 @@
     lines = jax.ShapeDtypeStruct((rows * blocks * 2, LANES), f32)
     view = object_layer_slices.reshape(rows, 2, blocks, LANES).transpose(0, 2, 1, 3)
     view = view.reshape(lines.shape)
-    dft = dft_block(side)
     own, recv = pl.pallas_call(
         main_kernel,
         out_shape=(window, window),
-        in_specs=[SMEM, SMEM, VMEM, HBM, VMEM, VMEM, VMEM, VMEM],
+        in_specs=[SMEM, SMEM, HBM, HBM, VMEM, VMEM, VMEM],
         out_specs=(VMEM, VMEM),
-        scratch_shapes=[pltpu.VMEM(tile_shape, bf16)] * 3
+        scratch_shapes=[pltpu.VMEM(lines.shape, f32)]
+        + [pltpu.VMEM((2 * side, 2 * side), bf16)] * 2
+        + [pltpu.VMEM(tile_shape, bf16)] * 3
         + [pltpu.VMEM(extent, f32)]
         + [pltpu.VMEM(window_shape, bf16)] * 4
         + [pltpu.VMEM((slots, side, side), f32)]
         + [pltpu.VMEM((2 * side, 2 * side), bf16)] * 2
         + [pltpu.SemaphoreType.DMA((2, CHUNKS))] * 2
         + [pltpu.SemaphoreType.DMA((2, slots))] * 2
-        + [pltpu.SemaphoreType.DMA],
+        + [pltpu.SemaphoreType.DMA((2,))],
         compiler_params=pltpu.CompilerParams(
-            collective_id=0, has_side_effects=True, vmem_limit_bytes=44 << 20
+            collective_id=0, has_side_effects=True, vmem_limit_bytes=49 << 20
         ),
         name="waves",
     )(
         positions, counts, view, measured, probe_wave.transpose(1, 0, 2),
-        propagator.transpose(1, 0, 2), jnp.asarray(dft), jnp.asarray(np.ascontiguousarray(dft.T)),
+        propagator.transpose(1, 0, 2), jnp.asarray(dft_planes(side)),
     )
     inner, near, far = pl.pallas_call(
         add_kernel,

time: 88.6 us -> 82.3 us (0.929)
  local copies, waits for them, and re-layouts: 9.26 us -> 4.8 us
  Pallas kernels: 79 us -> 77.3 us
    unnamed x12 -> x6, local copies, waits for them, and re-layouts: 8.16 us -> 3.69 us
    pallas_call x1, Pallas kernels: 42.8 us -> 41.4 us  [local(): pl.pallas_call(main_kernel, out_shape=(window, window), in_specs=[SMEM, S...]
where the time goes in v2:
time: 82.3 us; the launch traced here: 82.1 us
  Pallas kernels  77.3 us (94%)
  local copies, waits for them, and re-layouts  4.8 us (6%)
    pallas_call x1, Pallas kernels, local(): pl.pallas_call(main_kernel, out_shape=(window, window), in_specs=[SMEM, S...  41.4 us
    pallas_call x1, Pallas kernels, local(): pl.pallas_call(home_kernel, out_shape=lines, in_specs=[VMEM] * 3, out_spe...  33 us
    unnamed x6, local copies, waits for them, and re-layouts  3.69 us
    pallas_call x1, Pallas kernels, local(): pl.pallas_call(add_kernel, out_shape=(tile_f32, tile_bf16, tile_bf16), in...  2.95 us

profile of v2, /device:TPU:0, one launch (start us, length us, event | category | flops | bytes accessed | tf_op | source)
XLA Modules:
  0.0 82.1 jit_solution(6056343195233455482)
XLA Ops:
  0.0 0.8 copy.12.pos_ref
  0.8 1.1 %copy_bitcast_fusion = (bf16[2,256,256]{2,1,0:T(8,128)(2,1)S(1)}, bf16[2,256,256]{2,1,0:T(8,128)(2,1)S(1)}) fusion(bf16[256,2,256]{2,1,0:T(2,128)(2,1)} %param.9, bf16[256,2,256]{2,1,0:T(2,128)(2,1)} %param.8), kind=kLoop, calls=%fused_computation | loop fusion | bytes 1048576 | tf_op jit(solution)/shard_map/transpose | solution.py:420
  1.9 0.0 copy-start
  1.9 0.9 %copy-done = bf16[2,256,256]{2,1,0:T(8,128)(2,1)S(1)} copy-done((bf16[2,256,256]{2,1,0:T(8,128)(2,1)S(1)}, bf16[2,256,256]{2,1,0:T(8,128)(2,1)}, u32[]{:S(2)}) %copy-start) | copy-done | bytes 262168
  2.8 0.0 copy-start.1
  2.8 0.7 copy-done.1
  3.5 41.4 %waves.1 = (bf16[5,2,256,256]{3,2,1,0:T(8,128)(2,1)S(1)}, bf16[5,2,256,256]{3,2,1,0:T(8,128)(2,1)S(1)}) custom-call(s32[1,2,5,2]{3,2,1,0:T(8,128)S(1)} %copy.12.pos_ref, s32[1,2]{1,0:T(1,128)S(1)} %copy-done.1, f32[4096,128]{1,0:T(8,128)} %bitcast.15, f32[1,2,5,256,256]{4,3,2,1,0:T(8,128)} %meas_ref.1, bf16[2,256,256]{2,1,0:T(8,128)(2,1)S(1)} %get-tuple-element.16.probe_ref, ...), custom_call_target="tpu_custom_call" | custom-call | tf_op jit(solution)/shard_map/waves/pallas_call | solution.py:399
  44.9 3.0 %add.1 = (f32[16,2,128,128]{3,2,1,0:T(8,128)S(1)}, bf16[16,2,128,128]{3,2,1,0:T(8,128)(2,1)S(1)}, bf16[16,2,128,128]{3,2,1,0:T(8,128)(2,1)S(1)}) custom-call(s32[1,2,5,2]{3,2,1,0:T(8,128)S(1)} %copy.12.pos_ref, bf16[5,2,256,256]{3,2,1,0:T(8,128)(2,1)S(1)} %get-tuple-element.10.own_ref, bf16[5,2,256,256]{3,2,1,0:T(8,128)(2,1)S(1)} %get-tuple-element.11.recv_ref), custom_call_target="tpu_custom_call" | custom-call | tf_op jit(solution)/shard_map/add/pallas_call | solution.py:422
  47.8 33.0 %home.1 = f32[4096,128]{1,0:T(8,128)S(1)} custom-call(f32[16,2,128,128]{3,2,1,0:T(8,128)S(1)} %get-tuple-element.12.inner_ref, bf16[16,2,128,128]{3,2,1,0:T(8,128)(2,1)S(1)} %get-tuple-element.13.near_ref, bf16[16,2,128,128]{3,2,1,0:T(8,128)(2,1)S(1)} %get-tuple-element.14.far_ref), custom_call_target="tpu_custom_call" | custom-call | tf_op jit(solution)/shard_map/home/pallas_call | solution.py:431
  80.8 1.3 %copy.17 = f32[1,128,2,2048]{3,2,1,0:T(2,128)} copy(f32[1,128,2,2048]{3,2,1,0:T(2,128)S(1)} %bitcast.14) | data formatting | bytes 4194304
Async XLA Ops:
  1.9 1.0 %copy-start = (bf16[2,256,256]{2,1,0:T(8,128)(2,1)S(1)}, bf16[2,256,256]{2,1,0:T(8,128)(2,1)}, u32[]{:S(2)}) copy-start(bf16[2,256,256]{2,1,0:T(8,128)(2,1)} %constant.2.clone.fourier_ref) | copy-start | bytes 786436
  2.8 0.7 copy-start.1
